TPU v7x, 32 devices: a whole 2x2x4 slice. The times are simulated.
32 devices in a mesh: group: 2 (over y), user: 2 (over core), cand: 8 (over z, x).
Axes of the slice: x: 2, y: 2, z: 4, core: 2. Of those that a mesh axis runs over, the one named last changes fastest.
Arguments:
- history: bfloat16 [4, 1024, 1024], P(('group', 'user'), None, 'cand'), parts along dimension 0, may hold values from -6 to 6
- hist_len: int32 [4], P(('group', 'user')), parts along dimension 0, may hold values from 256 to 1024
- tile_counts: int32 [4, 8], P(('group', 'user'), 'cand'), parts along dimension 0, may hold values from 0 to 3, as said below
- cand_emb: bfloat16 [4, 3072, 1024], P(('group', 'user'), 'cand'), parts along dimension 0, may hold values from -3 to 3
- w_in: bfloat16 [1024, 4096], P(None, 'cand'), may hold values from -1 to 1
- out_gain: float32 [1024], replicated, may hold values from 0.25 to 1.75
- w_out: bfloat16 [1024, 1024], P(None, 'cand'), may hold values from -0.1875 to 0.1875
Outputs:
- cand_out: bfloat16 [4, 3072, 1024], P(('group', 'user'), 'cand'), parts along dimension 0
There are 2 independent parts, one for each index of `group`. A program takes and returns all parts, laid end to end along the dimension named above; an argument that names none is the same for every part. Nothing has to cross between parts.
Inputs may be any that keep to these rules, and one draw needn't show every extreme that they name: In each user's row of tile_counts exactly 1 entries equal 3, 2 * (1) entries are 0 and all others are 1, so that each row sums to its number of entries; which entries take which value is random.
All inputs are finite; a program needn't handle non-finite values.
Results may differ from a plain program's by a relative error of at most 0.0069.
Values may be sent and summed in bfloat16 or wider, within the bound.
A program may use at most 64 MiB of HBM per device.

v0:
```python
import math
import jax
import jax.numpy as jnp
from jax import lax
from jax.sharding import PartitionSpec as P

D = 1024
HEADS = 8
DH = 128
TILE = 128


def layer_norm(values):
    center = values - jnp.mean(values, axis=-1, keepdims=True)
    spread = jnp.mean(center * center, axis=-1, keepdims=True)
    return center * lax.rsqrt(spread + 1e-05)


def attend_rows(carry, kv_piece, queries, length, score_scale):
    key_count = kv_piece.shape[0]
    values = kv_piece[:, :D].reshape(key_count, HEADS, DH)
    key_heads = kv_piece[:, D:].reshape(key_count, HEADS, DH)
    scores = (
        jnp.einsum("rhe,the->hrt", queries, key_heads, preferred_element_type=jnp.float32)
        * score_scale
    )
    positions = jnp.arange(key_count, dtype=jnp.int32)
    weights = jnp.where(positions[None, None, :] < length, jax.nn.silu(scores), 0.0).astype(
        jnp.bfloat16
    )
    mixed_sum = jnp.einsum("hrt,the->rhe", weights, values, preferred_element_type=jnp.float32)
    return mixed_sum.reshape(carry.shape)


def score_rows(embedded, history, length, w_in, out_gain, w_out):
    score_scale = 1.0 / math.sqrt(DH)
    rows_here = embedded.shape[0]
    normed = layer_norm(embedded.astype(jnp.float32)).astype(jnp.bfloat16)
    initial = jnp.zeros((rows_here, D), jnp.float32)
    own_events = lax.all_to_all(history, "cand", split_axis=0, concat_axis=1, tiled=True)
    hist_normed = layer_norm(own_events.astype(jnp.float32)).astype(jnp.bfloat16)
    stacked = jnp.concatenate([normed, hist_normed], axis=0)
    projected = jax.nn.silu(
        jnp.dot(
            stacked,
            lax.all_gather(w_in, "cand", axis=1, tiled=True),
            preferred_element_type=jnp.float32,
        )
    ).astype(jnp.bfloat16)
    proj_rows = projected[:rows_here]
    hist_proj = projected[rows_here:]
    kv_local = jnp.concatenate([hist_proj[:, D : 2 * D], hist_proj[:, 3 * D :]], axis=1)
    queries = proj_rows[:, 2 * D : 3 * D].reshape(rows_here, HEADS, DH)
    summed = attend_rows(
        initial, lax.all_gather(kv_local, "cand", axis=0, tiled=True), queries, length, score_scale
    )
    gate_part = proj_rows[:, :D].astype(jnp.float32)
    cand_values = proj_rows[:, D : 2 * D].reshape(rows_here, HEADS, DH).astype(jnp.float32)
    cand_keys = proj_rows[:, 3 * D :].reshape(rows_here, HEADS, DH).astype(jnp.float32)
    own_score = jax.nn.silu(jnp.sum(queries.astype(jnp.float32) * cand_keys, axis=-1) * score_scale)
    attn = summed + (own_score[:, :, None] * cand_values).reshape(rows_here, D)
    gated = (layer_norm(attn) * out_gain[None, :] * gate_part).astype(jnp.bfloat16)
    residual = embedded.astype(jnp.float32)
    return (
        residual
        + jnp.dot(
            gated,
            lax.all_gather(w_out, "cand", axis=1, tiled=True),
            preferred_element_type=jnp.float32,
        )
    ).astype(jnp.bfloat16)


def shards(history, hist_len, tile_counts, cand_emb, w_in, out_gain, w_out):
    tile_total = tile_counts[0, 0]
    length = hist_len[0]
    slot_rows = cand_emb[0]
    slot_count = slot_rows.shape[0]
    own_history = history[0]
    scored = score_rows(slot_rows, own_history, length, w_in, out_gain, w_out)
    live = jnp.arange(slot_count, dtype=jnp.int32) < tile_total * TILE
    result = jnp.where(live[:, None], scored, jnp.zeros_like(scored))
    return result[None]


def solution(mesh):
    in_specs = (
        P(("group", "user"), None, "cand"),
        P(("group", "user")),
        P(("group", "user"), "cand"),
        P(("group", "user"), "cand", None),
        P(None, "cand"),
        P(),
        P(None, "cand"),
    )
    out_specs = P(("group", "user"), "cand", None)
    return jax.shard_map(shards, mesh=mesh, in_specs=in_specs, out_specs=out_specs, check_vma=False)
```

profile of v0, /device:TPU:0, one launch (start us, length us, event | category | flops | bytes accessed | tf_op | source)
XLA Modules:
  0.0 282.9 jit_solution(6100628635871063216)
XLA Ops:
  6.5 0.0 copy-start
  6.5 0.0 all-gather.4.cloned.1.call-start
  6.5 0.7 all-gather.4.cloned.1.call-update
  7.3 7.3 %all-to-all-start = ((bf16[8,128,128]{2,1,0:T(8,128)(2,1)}), bf16[8,128,128]{2,1,0:T(8,128)(2,1)S(1)}, u32[]{:S(2)}, u32[]{:S(2)}) async-start(bf16[8,128,128]{2,1,0:T(8,128)(2,1)} %bitcast.72), calls=%async_computation | async-start | bytes 524288 | tf_op jit(solution)/shard_map/all_to_all | solution.py:40
  14.5 0.0 all-gather.6.cloned.1.call-start
  14.6 0.0 copy-done
  14.6 0.2 convert_reduce_fusion
  14.8 0.3 fusion.11
  15.1 0.3 fusion.12
  15.4 8.1 %all-to-all-done = bf16[8,128,128]{2,1,0:T(8,128)(2,1)S(1)} async-done(((bf16[8,128,128]{2,1,0:T(8,128)(2,1)}), bf16[8,128,128]{2,1,0:T(8,128)(2,1)S(1)}, u32[]{:S(2)}, u32[]{:S(2)}) %all-to-all-start) | async-done | bytes 262176 | tf_op jit(solution)/shard_map/all_to_all | solution.py:40
  23.5 0.1 convert_reduce_fusion.1
  23.6 0.2 fusion.32
  23.8 0.2 fusion.34
  24.1 113.9 %all-gather.4.cloned.1.call-done = bf16[1024,4096]{1,0:T(8,128)(2,1)} async-done(((bf16[1024,512]{1,0:T(8,128)(2,1)}), bf16[1024,4096]{1,0:T(8,128)(2,1)}) %all-gather.4.cloned.1.call-update) | async-done | bytes 8388624 | tf_op jit(solution)/shard_map/all_gather | solution.py:46
  137.9 8.6 %multiply_convert_fusion = bf16[512,4096]{1,0:T(8,128)(2,1)S(1)} fusion(bf16[1024,4096]{1,0:T(8,128)(2,1)} %all-gather.4.cloned.1.call-done, bf16[128,1024]{1,0:T(8,128)(2,1)S(1)} %fusion.34, bf16[384,1024]{1,0:T(8,128)(2,1)S(1)} %fusion.12), kind=kOutput, calls=%fused_computation.1 | convolution fusion | flops 4307550208 | bytes 13631488 | tf_op jit(solution)/shard_map/dot_general | solution.py:44
  146.6 0.0 copy-start.2
  146.6 1.9 copy-done.2
  148.5 0.9 pad_maximum_fusion
  149.4 0.0 all-gather.6.cloned.1.call-update
  149.4 0.0 all-gather.8.cloned.1.call-start
  149.5 0.7 all-gather.8.cloned.1.call-update
  151.5 2.6 slice_bitcast_fusion.2
  154.1 0.3 copy.37
  154.4 0.2 copy.36
  154.6 0.5 multiply_reduce_fusion.1
  155.1 0.1 copy.29
  155.2 0.1 copy.30
  155.3 65.8 %all-gather.6.cloned.1.call-done = bf16[1024,2048]{1,0:T(8,128)(2,1)} async-done(((bf16[128,2048]{1,0:T(8,128)(2,1)}), bf16[1024,2048]{1,0:T(8,128)(2,1)}) %all-gather.6.cloned.1.call-update) | async-done | bytes 4194320 | tf_op jit(solution)/shard_map/all_gather | solution.py:55
  221.2 4.2 %slice_bitcast_fusion = (bf16[128,8,8,128]{3,2,1,0:T(8,128)(2,1)}, bf16[1024,1024]{1,0:T(8,128)(2,1)S(1)}) fusion(bf16[1024,2048]{1,0:T(8,128)(2,1)} %all-gather.6.cloned.1.call-done), kind=kLoop, calls=%fused_computation.6 | loop fusion | bytes 8388608
  225.4 2.6 copy.31
  227.9 7.5 %fusion = f32[8,128,384]{2,1,0:T(8,128)S(1)} fusion(bf16[1024,8,128]{0,2,1:T(8,128)(2,1)} %bitcast.70, pred[1024]{0:T(1024)(128)(4,1)S(1)} %iota_compare_fusion, bf16[128,8,8,128]{3,2,1,0:T(8,128)(2,1)} %get-tuple-element.10, bf16[48,8,8,128]{3,2,1,0:T(8,128)(2,1)} %get-tuple-element.8), kind=kOutput, calls=%fused_computation.2 | convolution fusion | flops 1632632832 | bytes 6554624 | tf_op jit(solution)/shard_map/hrt,the->rhe/dot_general | solution.py:31
  235.4 1.6 copy.32
  237.1 0.0 copy-start.1
  237.1 0.5 mul.114
  237.6 0.9 copy-done.1
  238.5 0.0 copy-start.3
  238.5 1.7 fusion.39
  240.2 0.3 multiply_reduce_fusion
  240.5 32.1 %all-gather.8.cloned.1.call-done = bf16[1024,1024]{1,0:T(8,128)(2,1)} async-done(((bf16[1024,128]{1,0:T(8,128)(2,1)}), bf16[1024,1024]{1,0:T(8,128)(2,1)}) %all-gather.8.cloned.1.call-update) | async-done | bytes 2097168 | tf_op jit(solution)/shard_map/all_gather | solution.py:68
  272.6 0.0 copy-done.3
  272.6 3.8 %fusion.16 = bf16[1,384,1024]{2,1,0:T(8,128)(2,1)} fusion(bf16[1024,1024]{1,0:T(8,128)(2,1)} %all-gather.8.cloned.1.call-done, bf16[1,384,1024]{2,1,0:T(8,128)(2,1)S(1)} %copy-done, f32[384,1024]{1,0:T(8,128)S(1)} %get-tuple-element.6, bf16[512,4096]{1,0:T(8,128)(2,1)} %copy-done.2, f32[1024]{0:T(1024)S(1)} %copy-done.3, f32[384]{0:T(512)S(1)} %add_rsqrt_fusion, ...), kind=kOutput, calls=%fused_computation.23 | convolution fusion | flops 809238528 | bytes 6036864 | tf_op jit(solution)/shard_map/dot_general | solution.py:66
  (10 shorter events, 0.1 us)
Async XLA Ops:
  6.5 8.0 %copy-start = (bf16[1,384,1024]{2,1,0:T(8,128)(2,1)S(1)}, bf16[1,384,1024]{2,1,0:T(8,128)(2,1)}, u32[]{:S(2)}) copy-start(bf16[1,384,1024]{2,1,0:T(8,128)(2,1)} %param.10) | copy-start | bytes 2359300
  6.5 131.4 %all-gather.4.cloned.1.call-start = ((), (), s32[]{:S(2)}) async-start(), calls=%async_computation.1 | async-start | bytes 9437184 | tf_op jit(solution)/shard_map/all_gather | solution.py:46
  7.3 16.2 %all-to-all-start = ((bf16[8,128,128]{2,1,0:T(8,128)(2,1)}), bf16[8,128,128]{2,1,0:T(8,128)(2,1)S(1)}, u32[]{:S(2)}, u32[]{:S(2)}) async-start(bf16[8,128,128]{2,1,0:T(8,128)(2,1)} %bitcast.72), calls=%async_computation | async-start | bytes 524288 | tf_op jit(solution)/shard_map/all_to_all | solution.py:40
  14.5 206.6 %all-gather.6.cloned.1.call-start = ((), (), s32[]{:S(2)}) async-start(), calls=%async_computation.2 | async-start | bytes 4718592 | tf_op jit(solution)/shard_map/all_gather | solution.py:55
  146.6 1.9 copy-start.2
  149.4 123.2 %all-gather.8.cloned.1.call-start = ((), (), s32[]{:S(2)}) async-start(), calls=%async_computation.3 | async-start | bytes 2359296 | tf_op jit(solution)/shard_map/all_gather | solution.py:68
  237.1 1.4 copy-start.1
  238.5 34.1 %copy-start.3 = (f32[1024]{0:T(1024)S(1)}, f32[1024]{0:T(1024)}, u32[]{:S(2)}) copy-start(f32[1024]{0:T(1024)} %param.12) | copy-start | bytes 12292
Sparse Core Ops, SparseCore 0:
  9.4 128.4 all-gather.3
  149.5 71.5 all-gather.5
  223.2 49.3 all-gather.7
where the time goes:
time: 283 us
  waiting for transfers between devices  221 us (78%)
  matrix products  19.9 us (7%)
  between operations  14.5 us (5%)
  local copies, waits for them, and re-layouts  12.5 us (4%)
  other arithmetic  7.38 us (3%)
  starting transfers between devices  7.35 us (3%)
    all_gather x1, waiting for transfers between devices, score_rows(): lax.all_gather(w_in, 'cand', axis=1, tiled=True)  114 us
    all_gather x1, waiting for transfers between devices, score_rows(): lax.all_gather(kv_local, 'cand', axis=0, tiled=True)  65.8 us
    all_gather x1, waiting for transfers between devices, score_rows(): lax.all_gather(w_out, 'cand', axis=1, tiled=True)  32.1 us
    dot_general x1, matrix products, score_rows(): jnp.dot(stacked, lax.all_gather(w_in, 'cand', axis=1, tiled=True), prefer...  8.61 us
    all_to_all x1, waiting for transfers between devices, score_rows(): lax.all_to_all(history, 'cand', split_axis=0, concat_axis=1, tiled=True)  8.08 us
    unnamed x11, local copies, waits for them, and re-layouts  7.59 us
    dot_general x1, matrix products, attend_rows(): jnp.einsum('hrt,the->rhe', weights, values, preferred_element_type=jnp.fl...  7.51 us
    all_to_all x1, starting transfers between devices, score_rows(): lax.all_to_all(history, 'cand', split_axis=0, concat_axis=1, tiled=True)  7.26 us
  transfers between devices with their start and end apart: 4, of which 4 were waited for; matrix products, arithmetic and copies ran while one was open for 8% of the time, Pallas kernels for 0%

commit v1 on v0

--- a/solution.py
+++ b/solution.py
@@ -8,6 +8,14 @@
 HEADS = 8
 DH = 128
 TILE = 128
+
+
+def handle_the_fields(q_in, group_axis):
+    taken_in = lax.axis_size(group_axis)
+    parts_out = jnp.split(q_in, taken_in, axis=0)
+    t_next = jnp.stack(parts_out)
+    v_now = lax.all_to_all(t_next, split_axis=0, axis_name=group_axis, concat_axis=0)
+    return jnp.concatenate(v_now, axis=1)
 
 
 def layer_norm(values):
@@ -37,7 +45,7 @@
     rows_here = embedded.shape[0]
     normed = layer_norm(embedded.astype(jnp.float32)).astype(jnp.bfloat16)
     initial = jnp.zeros((rows_here, D), jnp.float32)
-    own_events = lax.all_to_all(history, "cand", split_axis=0, concat_axis=1, tiled=True)
+    own_events = handle_the_fields(history, "cand")
     hist_normed = layer_norm(own_events.astype(jnp.float32)).astype(jnp.bfloat16)
     stacked = jnp.concatenate([normed, hist_normed], axis=0)
     projected = jax.nn.silu(

time: 283 us -> 292 us (1.032)
  local copies, waits for them, and re-layouts: 12.5 us -> 23.5 us
  waiting for transfers between devices: 221 us -> 218 us
    unnamed x11 -> x18, local copies, waits for them, and re-layouts: 7.59 us -> 17.2 us
    all_gather x1, waiting for transfers between devices: 114 us -> 105 us  [score_rows(): lax.all_gather(w_in, 'cand', axis=1, tiled=True)]
    all_to_all x1, waiting for transfers between devices: 8.08 us -> 13.4 us  [handle_the_fields(): lax.all_to_all(t_next, split_axis=0, axis_name=group_axis, concat_axis=0)]
  transfers between devices with their start and end apart: 4 -> 4, of which waited for: 4 -> 4; matrix products, arithmetic and copies ran while one was open for 8% -> 12% of each run, Pallas kernels for 0% -> 0%
where the time goes in v1:
time: 292 us; the launch traced here: 291 us
  waiting for transfers between devices  218 us (75%)
  local copies, waits for them, and re-layouts  23.5 us (8%)
  matrix products  19.9 us (7%)
  between operations  14.5 us (5%)
  other arithmetic  7.38 us (3%)
  starting transfers between devices  7.34 us (3%)
    all_gather x1, waiting for transfers between devices, score_rows(): lax.all_gather(w_in, 'cand', axis=1, tiled=True)  105 us
    all_gather x1, waiting for transfers between devices, score_rows(): lax.all_gather(kv_local, 'cand', axis=0, tiled=True)  65.8 us
    all_gather x1, waiting for transfers between devices, score_rows(): lax.all_gather(w_out, 'cand', axis=1, tiled=True)  32.1 us
    unnamed x18, local copies, waits for them, and re-layouts  17.2 us
    all_to_all x1, waiting for transfers between devices, handle_the_fields(): lax.all_to_all(t_next, split_axis=0, axis_name=group_axis, concat_axis=0)  13.4 us
    dot_general x1, matrix products, score_rows(): jnp.dot(stacked, lax.all_gather(w_in, 'cand', axis=1, tiled=True), prefer...  8.61 us
    dot_general x1, matrix products, attend_rows(): jnp.einsum('hrt,the->rhe', weights, values, preferred_element_type=jnp.fl...  7.5 us
    all_to_all x1, starting transfers between devices, handle_the_fields(): lax.all_to_all(t_next, split_axis=0, axis_name=group_axis, concat_axis=0)  7.26 us
  transfers between devices with their start and end apart: 4, of which 4 were waited for; matrix products, arithmetic and copies ran while one was open for 12% of the time, Pallas kernels for 0%

profile of v1, /device:TPU:0, one launch (start us, length us, event | category | flops | bytes accessed | tf_op | source)
XLA Modules:
  0.0 290.7 jit_solution(741709542393272599)
XLA Ops:
  6.5 0.0 copy-start
  6.5 0.0 all-gather.4.cloned.1.call-start
  6.5 0.7 all-gather.4.cloned.1.call-update
  7.3 1.4 slice_dynamic-update-slice_fusion.7
  8.6 1.4 slice_dynamic-update-slice_fusion.6
  10.0 1.4 slice_dynamic-update-slice_fusion.5
  11.4 1.4 slice_dynamic-update-slice_fusion.4
  12.8 1.4 slice_dynamic-update-slice_fusion.3
  14.1 1.4 slice_dynamic-update-slice_fusion.2
  15.5 1.4 slice_dynamic-update-slice_fusion.1
  16.9 1.4 slice_dynamic-update-slice_fusion
  18.3 7.3 %all-to-all-start = ((bf16[8,128,128]{2,1,0:T(8,128)(2,1)}), bf16[8,128,128]{2,1,0:T(8,128)(2,1)S(1)}, u32[]{:S(2)}, u32[]{:S(2)}) async-start(bf16[8,128,128]{2,1,0:T(8,128)(2,1)} %slice_dynamic-update-slice_fusion), calls=%async_computation | async-start | bytes 524288 | tf_op jit(solution)/shard_map/all_to_all | solution.py:17
  25.5 0.0 all-gather.6.cloned.1.call-start
  25.6 0.0 copy-done
  25.6 0.2 convert_reduce_fusion
  25.8 0.3 fusion.11
  26.1 0.3 fusion.12
  26.4 13.4 %all-to-all-done = bf16[8,128,128]{2,1,0:T(8,128)(2,1)S(1)} async-done(((bf16[8,128,128]{2,1,0:T(8,128)(2,1)}), bf16[8,128,128]{2,1,0:T(8,128)(2,1)S(1)}, u32[]{:S(2)}, u32[]{:S(2)}) %all-to-all-start) | async-done | bytes 262176 | tf_op jit(solution)/shard_map/all_to_all | solution.py:17
  39.8 0.1 convert_reduce_fusion.1
  39.9 0.2 fusion.32
  40.2 0.2 fusion.34
  40.4 105.3 %all-gather.4.cloned.1.call-done = bf16[1024,4096]{1,0:T(8,128)(2,1)} async-done(((bf16[1024,512]{1,0:T(8,128)(2,1)}), bf16[1024,4096]{1,0:T(8,128)(2,1)}) %all-gather.4.cloned.1.call-update) | async-done | bytes 8388624 | tf_op jit(solution)/shard_map/all_gather | solution.py:54
  145.7 8.6 %multiply_convert_fusion = bf16[512,4096]{1,0:T(8,128)(2,1)S(1)} fusion(bf16[1024,4096]{1,0:T(8,128)(2,1)} %all-gather.4.cloned.1.call-done, bf16[128,1024]{1,0:T(8,128)(2,1)S(1)} %fusion.34, bf16[384,1024]{1,0:T(8,128)(2,1)S(1)} %fusion.12), kind=kOutput, calls=%fused_computation.1 | convolution fusion | flops 4307550208 | bytes 13631488 | tf_op jit(solution)/shard_map/dot_general | solution.py:52
  154.3 0.0 copy-start.2
  154.3 1.9 copy-done.2
  156.3 0.9 pad_maximum_fusion
  157.1 0.0 all-gather.6.cloned.1.call-update
  157.2 0.0 all-gather.8.cloned.1.call-start
  157.2 0.7 all-gather.8.cloned.1.call-update
  159.2 2.6 slice_bitcast_fusion.2
  161.8 0.3 copy.32
  162.2 0.2 copy.31
  162.3 0.5 multiply_reduce_fusion.1
  162.8 0.1 copy.24
  163.0 0.1 copy.25
  163.1 65.8 %all-gather.6.cloned.1.call-done = bf16[1024,2048]{1,0:T(8,128)(2,1)} async-done(((bf16[128,2048]{1,0:T(8,128)(2,1)}), bf16[1024,2048]{1,0:T(8,128)(2,1)}) %all-gather.6.cloned.1.call-update) | async-done | bytes 4194320 | tf_op jit(solution)/shard_map/all_gather | solution.py:63
  228.9 4.2 %slice_bitcast_fusion = (bf16[128,8,8,128]{3,2,1,0:T(8,128)(2,1)}, bf16[1024,1024]{1,0:T(8,128)(2,1)S(1)}) fusion(bf16[1024,2048]{1,0:T(8,128)(2,1)} %all-gather.6.cloned.1.call-done), kind=kLoop, calls=%fused_computation.6 | loop fusion | bytes 8388608
  233.1 2.6 copy.26
  235.7 7.5 %fusion = f32[8,128,384]{2,1,0:T(8,128)S(1)} fusion(bf16[1024,8,128]{0,2,1:T(8,128)(2,1)} %bitcast.69, pred[1024]{0:T(1024)(128)(4,1)S(1)} %iota_compare_fusion, bf16[128,8,8,128]{3,2,1,0:T(8,128)(2,1)} %get-tuple-element.10, bf16[48,8,8,128]{3,2,1,0:T(8,128)(2,1)} %get-tuple-element.8), kind=kOutput, calls=%fused_computation.2 | convolution fusion | flops 1632632832 | bytes 6554624 | tf_op jit(solution)/shard_map/hrt,the->rhe/dot_general | solution.py:39
  243.2 1.6 copy.27
  244.8 0.5 mul.114
  245.3 0.9 copy-done.1
  246.3 0.0 copy-start.3
  246.3 1.7 fusion.39
  247.9 0.3 multiply_reduce_fusion
  248.2 32.1 %all-gather.8.cloned.1.call-done = bf16[1024,1024]{1,0:T(8,128)(2,1)} async-done(((bf16[1024,128]{1,0:T(8,128)(2,1)}), bf16[1024,1024]{1,0:T(8,128)(2,1)}) %all-gather.8.cloned.1.call-update) | async-done | bytes 2097168 | tf_op jit(solution)/shard_map/all_gather | solution.py:76
  280.4 0.0 copy-done.3
  280.4 3.8 %fusion.16 = bf16[1,384,1024]{2,1,0:T(8,128)(2,1)} fusion(bf16[1024,1024]{1,0:T(8,128)(2,1)} %all-gather.8.cloned.1.call-done, bf16[1,384,1024]{2,1,0:T(8,128)(2,1)S(1)} %copy-done, f32[384,1024]{1,0:T(8,128)S(1)} %get-tuple-element.6, bf16[512,4096]{1,0:T(8,128)(2,1)} %copy-done.2, f32[1024]{0:T(1024)S(1)} %copy-done.3, f32[384]{0:T(512)S(1)} %add_rsqrt_fusion, ...), kind=kOutput, calls=%fused_computation.23 | convolution fusion | flops 809238528 | bytes 6036864 | tf_op jit(solution)/shard_map/dot_general | solution.py:74
  (11 shorter events, 0.1 us)
Async XLA Ops:
  6.5 19.0 %copy-start = (bf16[1,384,1024]{2,1,0:T(8,128)(2,1)S(1)}, bf16[1,384,1024]{2,1,0:T(8,128)(2,1)}, u32[]{:S(2)}) copy-start(bf16[1,384,1024]{2,1,0:T(8,128)(2,1)} %param.10) | copy-start | bytes 2359300
  6.5 139.2 %all-gather.4.cloned.1.call-start = ((), (), s32[]{:S(2)}) async-start(), calls=%async_computation.1 | async-start | bytes 9437184 | tf_op jit(solution)/shard_map/all_gather | solution.py:54
  18.3 21.5 %all-to-all-start = ((bf16[8,128,128]{2,1,0:T(8,128)(2,1)}), bf16[8,128,128]{2,1,0:T(8,128)(2,1)S(1)}, u32[]{:S(2)}, u32[]{:S(2)}) async-start(bf16[8,128,128]{2,1,0:T(8,128)(2,1)} %slice_dynamic-update-slice_fusion), calls=%async_computation | async-start | bytes 524288 | tf_op jit(solution)/shard_map/all_to_all | solution.py:17
  25.5 203.4 %all-gather.6.cloned.1.call-start = ((), (), s32[]{:S(2)}) async-start(), calls=%async_computation.2 | async-start | bytes 4718592 | tf_op jit(solution)/shard_map/all_gather | solution.py:63
  154.3 1.9 copy-start.2
  157.2 123.2 %all-gather.8.cloned.1.call-start = ((), (), s32[]{:S(2)}) async-start(), calls=%async_computation.3 | async-start | bytes 2359296 | tf_op jit(solution)/shard_map/all_gather | solution.py:76
  244.8 1.4 copy-start.1
  246.3 34.1 %copy-start.3 = (f32[1024]{0:T(1024)S(1)}, f32[1024]{0:T(1024)}, u32[]{:S(2)}) copy-start(f32[1024]{0:T(1024)} %param.12) | copy-start | bytes 12292
Sparse Core Ops, SparseCore 0:
  9.4 136.2 all-gather.3
  157.3 71.5 all-gather.5
  231.0 49.3 all-gather.7
